TPU v7x, 32 devices: a whole 2x2x4 slice. The times are simulated.
32 devices in a mesh: dp: 8 (over y, x, core), tensor: 4 (over z).
Axes of the slice: x: 2, y: 2, z: 4, core: 2. Of those that a mesh axis runs over, the one named last changes fastest.
Arguments:
- inputs: bfloat16 [2048, 2048], P(('dp', 'tensor')), parts along dimension 0, may hold values from -6 to 6
- grad_out: bfloat16 [2048, 2048], P(('dp', 'tensor')), parts along dimension 0, may hold values from -6 to 6
- gate_weight: bfloat16 [2048, 7168], P(None, 'tensor'), may hold values from -6 to 6
- up_weight: bfloat16 [2048, 7168], P(None, 'tensor'), may hold values from -6 to 6
- down_weight: bfloat16 [7168, 2048], P('tensor'), may hold values from -6 to 6
Outputs:
- grad_inputs: bfloat16 [2048, 2048], P(('dp', 'tensor')), parts along dimension 0
- grad_gate: bfloat16 [16384, 7168], P('dp', 'tensor'), parts along dimension 0
- grad_up: bfloat16 [16384, 7168], P('dp', 'tensor'), parts along dimension 0
- grad_down: bfloat16 [57344, 2048], P(('dp', 'tensor')), parts along dimension 0
There are 8 independent parts, one for each index of `dp`. A program takes and returns all parts, laid end to end along the dimension named above; an argument that names none is the same for every part. Nothing has to cross between parts.
All inputs are finite; a program needn't handle non-finite values.
Results may differ from a plain program's by a relative error of at most 0.0049.
Values may be sent and summed in bfloat16 or wider, within the bound.
A program may use at most 128 MiB of HBM per device.

v0:
```python
import jax
import jax.numpy as jnp
from jax import lax
from jax.sharding import PartitionSpec as P

D = 2048
FF = 7168


def contract_last(left, right):
    return lax.dot_general(
        left, right, (((1,), (1,)), ((), ())), preferred_element_type=jnp.float32
    )


def contract_first(left, right):
    return lax.dot_general(
        left, right, (((0,), (0,)), ((), ())), preferred_element_type=jnp.float32
    )


def on_device(inputs, grad_out, gate_weight, up_weight, down_weight):
    tokens_all = lax.all_gather(inputs, "tensor", axis=0, tiled=True)
    grads_all = lax.all_gather(grad_out, "tensor", axis=0, tiled=True)
    inv_width = D ** (-0.5)
    inv_rows = tokens_all.shape[0] ** (-0.5)
    inv_hidden = (2 * FF) ** (-0.5)
    gate = jnp.dot(tokens_all, gate_weight, preferred_element_type=jnp.float32) * inv_width
    up = jnp.dot(tokens_all, up_weight, preferred_element_type=jnp.float32) * inv_width
    sig = jax.nn.sigmoid(gate)
    act = gate * sig
    hidden = (act * up).astype(jnp.bfloat16)
    d_hidden = contract_last(grads_all, down_weight) * inv_width
    grad_down = (contract_first(hidden, grads_all) * inv_rows).astype(jnp.bfloat16)
    d_gate = (d_hidden * up * sig * (1.0 + gate * (1.0 - sig))).astype(jnp.bfloat16)
    d_up = (d_hidden * act).astype(jnp.bfloat16)
    grad_gate = (contract_first(tokens_all, d_gate) * inv_rows).astype(jnp.bfloat16)
    grad_up = (contract_first(tokens_all, d_up) * inv_rows).astype(jnp.bfloat16)
    summed = lax.psum_scatter(
        contract_last(d_gate, gate_weight) * inv_hidden
        + contract_last(d_up, up_weight) * inv_hidden,
        "tensor",
        scatter_dimension=0,
        tiled=True,
    )
    grad_inputs = summed.astype(jnp.bfloat16)
    return (grad_inputs, grad_gate, grad_up, grad_down)


def solution(mesh):
    placed = (
        P(("dp", "tensor"), None),
        P(("dp", "tensor"), None),
        P(None, "tensor"),
        P(None, "tensor"),
        P("tensor", None),
    )
    return jax.shard_map(
        on_device,
        mesh=mesh,
        in_specs=placed,
        out_specs=(
            P(("dp", "tensor"), None),
            P("dp", "tensor"),
            P("dp", "tensor"),
            P(("dp", "tensor"), None),
        ),
        check_vma=False,
    )
```

profile of v0, /device:TPU:0, one launch (start us, length us, event | category | flops | bytes accessed | tf_op | source)
XLA Modules:
  0.0 139.9 jit_solution(8619819542554499196)
XLA Ops:
  7.2 0.0 all-gather.5.cloned.1.call-start
  7.2 0.7 all-gather.5.cloned.1.call-update
  7.9 0.0 all-gather.3.cloned.1.call-start
  7.9 0.7 all-gather.3.cloned.1.call-update
  8.6 0.0 reduce-scatter.2.cloned.1.call-start
  8.7 31.5 %all-gather.5.cloned.1.call-done = bf16[256,2048]{1,0:T(8,128)(2,1)} async-done(((bf16[64,2048]{1,0:T(8,128)(2,1)}), bf16[256,2048]{1,0:T(8,128)(2,1)}) %all-gather.5.cloned.1.call-update) | async-done | bytes 1048592 | tf_op jit(solution)/shard_map/all_gather | solution.py:23
  40.2 0.0 copy-start
  40.2 6.8 %convolution_multiply_fusion = f32[256,1792]{1,0:T(8,128)} fusion(bf16[256,2048]{1,0:T(8,128)(2,1)} %all-gather.5.cloned.1.call-done, bf16[2048,1792]{1,0:T(8,128)(2,1)} %param.7), kind=kOutput, calls=%fused_computation.5 | convolution fusion | flops 1879506944 | bytes 10223616 | tf_op jit(solution)/shard_map/dot_general | solution.py:28
  47.0 0.0 copy-done
  47.0 6.6 %convolution_multiply_fusion.1 = f32[256,1792]{1,0:T(8,128)} fusion(bf16[256,2048]{1,0:T(8,128)(2,1)S(1)} %copy-done, bf16[2048,1792]{1,0:T(8,128)(2,1)} %param.8), kind=kOutput, calls=%fused_computation.6 | convolution fusion | flops 1879506944 | bytes 10223616 | tf_op jit(solution)/shard_map/dot_general | solution.py:29
  53.6 15.6 %all-gather.3.cloned.1.call-done = bf16[256,2048]{1,0:T(8,128)(2,1)} async-done(((bf16[64,2048]{1,0:T(8,128)(2,1)}), bf16[256,2048]{1,0:T(8,128)(2,1)}) %all-gather.3.cloned.1.call-update) | async-done | bytes 1048592 | tf_op jit(solution)/shard_map/all_gather | solution.py:24
  69.3 7.1 %multiply_convert_fusion.4 = (bf16[256,1792]{1,0:T(8,128)(2,1)S(1)}, bf16[256,1792]{1,0:T(8,128)(2,1)S(1)}) fusion(f32[256,1792]{1,0:T(8,128)} %convolution_multiply_fusion, f32[256,1792]{1,0:T(8,128)} %convolution_multiply_fusion.1, bf16[256,2048]{1,0:T(8,128)(2,1)} %all-gather.3.cloned.1.call-done, bf16[1792,2048]{1,0:T(8,128)(2,1)} %param.9), kind=kOutput, calls=%fused_computation.11 | convolution fusion | flops 1885470720 | bytes 13893632 | tf_op jit(solution)/shard_map/dot_general | solution.py:11
  76.3 5.2 %fusion.6 = f32[256,2048]{1,0:T(8,128)S(1)} fusion(bf16[256,1792]{1,0:T(8,128)(2,1)S(1)} %get-tuple-element.9, bf16[2048,1792]{1,0:T(8,128)(2,1)} %param.7), kind=kOutput, calls=%fused_computation.16 | convolution fusion | flops 1879048192 | bytes 10354688 | tf_op jit(solution)/shard_map/dot_general | solution.py:11
  81.5 6.6 %fusion.2 = f32[256,2048]{1,0:T(8,128)} fusion(f32[256,2048]{1,0:T(8,128)S(1)} %fusion.6, bf16[256,1792]{1,0:T(8,128)(2,1)S(1)} %get-tuple-element.8, bf16[2048,1792]{1,0:T(8,128)(2,1)} %param.8), kind=kOutput, calls=%fused_computation.9 | convolution fusion | flops 1880096768 | bytes 12451840 | tf_op jit(solution)/shard_map/dot_general | solution.py:11
  88.1 0.0 reduce-scatter.2.cloned.1.call-update
  88.1 5.2 %fusion.1 = bf16[2048,1792]{0,1:T(8,128)(2,1)} fusion(bf16[256,1792]{1,0:T(8,128)(2,1)S(1)} %get-tuple-element.8, bf16[256,2048]{1,0:T(8,128)(2,1)S(1)} %copy-done), kind=kOutput, calls=%fused_computation.4 | convolution fusion | flops 1886388224 | bytes 9306112 | tf_op jit(solution)/shard_map/dot_general | solution.py:17
  93.2 10.1 %copy.10 = bf16[2048,1792]{1,0:T(8,128)(2,1)} copy(bf16[2048,1792]{0,1:T(8,128)(2,1)} %fusion.1) | data formatting | bytes 14680064
  103.3 5.1 %fusion = bf16[2048,1792]{0,1:T(8,128)(2,1)} fusion(bf16[256,1792]{1,0:T(8,128)(2,1)S(1)} %get-tuple-element.9, bf16[256,2048]{1,0:T(8,128)(2,1)S(1)} %copy-done), kind=kOutput, calls=%fused_computation.3 | convolution fusion | flops 1886388224 | bytes 9306112 | tf_op jit(solution)/shard_map/dot_general | solution.py:17
  108.5 10.1 %copy.9 = bf16[2048,1792]{1,0:T(8,128)(2,1)} copy(bf16[2048,1792]{0,1:T(8,128)(2,1)} %fusion) | data formatting | bytes 14680064
  118.6 0.0 copy-done.1
  118.6 0.0 copy-done.2
  118.6 6.8 %multiply_convert_fusion = bf16[1792,2048]{1,0:T(8,128)(2,1)} fusion(bf16[256,2048]{1,0:T(8,128)(2,1)S(1)} %copy-done.1, f32[256,1792]{1,0:T(8,128)} %convolution_multiply_fusion.1, f32[256,1792]{1,0:T(8,128)S(1)} %copy-done.2), kind=kOutput, calls=%fused_computation | convolution fusion | flops 1889140736 | bytes 12058624 | tf_op jit(solution)/shard_map/dot_general | solution.py:17
  125.4 6.2 %reduce-scatter.2.cloned.1.call-done = f32[64,2048]{1,0:T(8,128)} async-done(((f32[256,2048]{1,0:T(8,128)}), f32[64,2048]{1,0:T(8,128)}) %reduce-scatter.2.cloned.1.call-update) | async-done | bytes 524304 | tf_op jit(solution)/shard_map/reduce_scatter | solution.py:39
  131.6 1.8 %convert_element_type.29 = bf16[64,2048]{1,0:T(8,128)(2,1)} convert(f32[64,2048]{1,0:T(8,128)} %reduce-scatter.2.cloned.1.call-done) | non-fusion elementwise | flops 131072 | bytes 786432 | tf_op jit(solution)/shard_map/convert_element_type | solution.py:46
  (2 shorter events, 0.0 us)
Async XLA Ops:
  7.2 33.1 %all-gather.5.cloned.1.call-start = ((), (), s32[]{:S(2)}) async-start(), calls=%async_computation.2 | async-start | bytes 1310720 | tf_op jit(solution)/shard_map/all_gather | solution.py:23
  7.9 61.4 %all-gather.3.cloned.1.call-start = ((), (), s32[]{:S(2)}) async-start(), calls=%async_computation.1 | async-start | bytes 1310720 | tf_op jit(solution)/shard_map/all_gather | solution.py:24
  8.6 122.9 %reduce-scatter.2.cloned.1.call-start = ((), (), s32[]{:S(2)}) async-start(), calls=%async_computation.3 | async-start | bytes 2621440 | tf_op jit(solution)/shard_map/reduce_scatter | solution.py:39
  40.2 6.8 %copy-start = (bf16[256,2048]{1,0:T(8,128)(2,1)S(1)}, bf16[256,2048]{1,0:T(8,128)(2,1)}, u32[]{:S(2)}) copy-start(bf16[256,2048]{1,0:T(8,128)(2,1)} %all-gather.5.cloned.1.call-done) | copy-start | bytes 3145732
  108.5 10.1 %copy-start.1 = (bf16[256,2048]{1,0:T(8,128)(2,1)S(1)}, bf16[256,2048]{1,0:T(8,128)(2,1)}, u32[]{:S(2)}) copy-start(bf16[256,2048]{1,0:T(8,128)(2,1)} %all-gather.3.cloned.1.call-done) | copy-start | bytes 3145732
  108.5 10.1 %copy-start.2 = (f32[256,1792]{1,0:T(8,128)S(1)}, f32[256,1792]{1,0:T(8,128)}, u32[]{:S(2)}) copy-start(f32[256,1792]{1,0:T(8,128)} %convolution_multiply_fusion) | copy-start | bytes 5505028
Sparse Core Ops, SparseCore 0:
  9.6 30.6 all-gather.4
  41.8 27.4 all-gather.2
  88.2 43.3 reduce-scatter.1
where the time goes:
time: 141 us; the launch traced here: 140 us
  waiting for transfers between devices  54.7 us (39%)
  matrix products  49.3 us (35%)
  local copies, waits for them, and re-layouts  20.2 us (14%)
  between operations  13.8 us (10%)
  other arithmetic  1.77 us (1%)
    all_gather x1, waiting for transfers between devices, on_device(): tokens_all = lax.all_gather(inputs, 'tensor', axis=0, tiled=True)  31.5 us
    unnamed x8, local copies, waits for them, and re-layouts  20.2 us
    dot_general x3, matrix products, contract_last(): lax.dot_general(left, right, (((1,), (1,)), ((), ())), preferred_element_...  18.8 us
    dot_general x3, matrix products, contract_first(): lax.dot_general(left, right, (((0,), (0,)), ((), ())), preferred_element_...  17.1 us
    all_gather x1, waiting for transfers between devices, on_device(): grads_all = lax.all_gather(grad_out, 'tensor', axis=0, tiled=True)  15.6 us
    dot_general x1, matrix products, on_device(): jnp.dot(tokens_all, gate_weight, preferred_element_type=jnp.float32)  6.77 us
    dot_general x1, matrix products, on_device(): jnp.dot(tokens_all, up_weight, preferred_element_type=jnp.float32)  6.64 us
    reduce_scatter x1, waiting for transfers between devices, on_device(): lax.psum_scatter(contract_last(d_gate, gate_weight) * inv_hidden + contra...  6.19 us
  transfers between devices with their start and end apart: 3, of which 3 were waited for; matrix products, arithmetic and copies ran while one was open for 36% of the time, Pallas kernels for 0%

commit v1 on v0

--- a/solution.py
+++ b/solution.py
@@ -20,8 +20,11 @@
 
 
 def on_device(inputs, grad_out, gate_weight, up_weight, down_weight):
-    tokens_all = lax.all_gather(inputs, "tensor", axis=0, tiled=True)
-    grads_all = lax.all_gather(grad_out, "tensor", axis=0, tiled=True)
+    tokens_all, grads_all = jnp.split(
+        lax.all_gather(jnp.concatenate([inputs, grad_out], axis=1), "tensor", axis=0, tiled=True),
+        [inputs.shape[1]],
+        axis=1,
+    )
     inv_width = D ** (-0.5)
     inv_rows = tokens_all.shape[0] ** (-0.5)
     inv_hidden = (2 * FF) ** (-0.5)

time: 141 us -> 136 us (0.965)
  waiting for transfers between devices: 54.7 us -> 76.5 us
  local copies, waits for them, and re-layouts: 20.2 us -> 0.04 us
  matrix products: 49.3 us -> 41.7 us
  other arithmetic: 1.77 us -> 3.63 us
    reduce_scatter x1, waiting for transfers between devices: 6.19 us -> 26.8 us  [on_device(): lax.psum_scatter(contract_last(d_gate, gate_weight) * inv_hidden + contra...]
    unnamed x8 -> x20, local copies, waits for them, and re-layouts: 20.2 us -> 0.04 us
    dot_general x3, matrix products: 18.8 us -> 12.5 us  [contract_last(): lax.dot_general(left, right, (((1,), (1,)), ((), ())), preferred_element_...]
    all_gather x2 -> x1, waiting for transfers between devices: 47.1 us -> 49.7 us  [on_device(): lax.all_gather(jnp.concatenate([inputs, grad_out], axis=1), 'tensor', axi...]
    concatenate x0 -> x1, other arithmetic: none -> 1.86 us  [on_device(): jnp.concatenate([inputs, grad_out], axis=1)]
  transfers between devices with their start and end apart: 3 -> 2, of which waited for: 3 -> 2; matrix products, arithmetic and copies ran while one was open for 36% -> 12% of each run, Pallas kernels for 0% -> 0%
where the time goes in v1:
time: 136 us
  waiting for transfers between devices  76.5 us (56%)
  matrix products  41.7 us (31%)
  between operations  14.1 us (10%)
  other arithmetic  3.63 us (3%)
    all_gather x1, waiting for transfers between devices, on_device(): lax.all_gather(jnp.concatenate([inputs, grad_out], axis=1), 'tensor', axi...  49.7 us
    reduce_scatter x1, waiting for transfers between devices, on_device(): lax.psum_scatter(contract_last(d_gate, gate_weight) * inv_hidden + contra...  26.8 us
    dot_general x3, matrix products, contract_first(): lax.dot_general(left, right, (((0,), (0,)), ((), ())), preferred_element_...  15.9 us
    dot_general x3, matrix products, contract_last(): lax.dot_general(left, right, (((1,), (1,)), ((), ())), preferred_element_...  12.5 us
    dot_general x1, matrix products, on_device(): jnp.dot(tokens_all, gate_weight, preferred_element_type=jnp.float32)  6.84 us
    dot_general x1, matrix products, on_device(): jnp.dot(tokens_all, up_weight, preferred_element_type=jnp.float32)  6.51 us
  transfers between devices with their start and end apart: 2, of which 2 were waited for; matrix products, arithmetic and copies ran while one was open for 12% of the time, Pallas kernels for 0%

profile of v1, /device:TPU:0, one launch (start us, length us, event | category | flops | bytes accessed | tf_op | source)
XLA Modules:
  0.0 136.1 jit_solution(15537065447585243660)
XLA Ops:
  7.2 0.0 all-gather.2.cloned.1.call-start
  7.2 1.9 %pad_maximum_fusion = bf16[64,4096]{1,0:T(8,128)(2,1)} fusion(bf16[64,2048]{1,0:T(8,128)(2,1)} %param.6, bf16[64,2048]{1,0:T(8,128)(2,1)} %param.5), kind=kLoop, calls=%fused_computation.19 | loop fusion | flops 1048576 | bytes 1048576 | tf_op jit(solution)/shard_map/concatenate | solution.py:24
  9.1 0.0 all-gather.2.cloned.1.call-update
  9.1 0.0 reduce-scatter.2.cloned.1.call-start
  9.1 49.7 %all-gather.2.cloned.1.call-done = bf16[256,4096]{1,0:T(8,128)(2,1)} async-done(((bf16[64,4096]{1,0:T(8,128)(2,1)}), bf16[256,4096]{1,0:T(8,128)(2,1)}) %all-gather.2.cloned.1.call-update) | async-done | bytes 2097168 | tf_op jit(solution)/shard_map/all_gather | solution.py:24
  58.8 6.8 %convolution_multiply_fusion = f32[256,1792]{1,0:T(8,128)} fusion(bf16[2048,1792]{1,0:T(8,128)(2,1)} %param.7, bf16[256,4096]{1,0:T(8,128)(2,1)} %all-gather.2.cloned.1.call-done), kind=kOutput, calls=%fused_computation.3 | convolution fusion | flops 1879506944 | bytes 10223616 | tf_op jit(solution)/shard_map/dot_general | solution.py:31
  65.7 0.0 copy-done
  65.7 6.5 %convolution_multiply_fusion.1 = f32[256,1792]{1,0:T(8,128)} fusion(bf16[2048,1792]{1,0:T(8,128)(2,1)} %param.8, bf16[256,4096]{1,0:T(8,128)(2,1)S(1)} %copy-done), kind=kOutput, calls=%fused_computation.4 | convolution fusion | flops 1879506944 | bytes 10223616 | tf_op jit(solution)/shard_map/dot_general | solution.py:32
  72.2 0.0 slice-done
  72.2 0.0 slice-done.1
  72.2 0.0 slice-start.5
  72.2 5.8 %multiply_convert_fusion.4 = (bf16[256,1792]{1,0:T(8,128)(2,1)S(1)}, bf16[256,1792]{1,0:T(8,128)(2,1)}) fusion(f32[256,1792]{1,0:T(8,128)} %convolution_multiply_fusion, f32[256,1792]{1,0:T(8,128)} %convolution_multiply_fusion.1, bf16[1792,2048]{1,0:T(8,128)(2,1)S(1)} %bitcast.10, bf16[256,4096]{1,0:T(8,128)(2,1)S(1)} %copy-done), kind=kOutput, calls=%fused_computation.9 | convolution fusion | flops 1885470720 | bytes 13893632 | tf_op jit(solution)/shard_map/dot_general | solution.py:11
  78.0 0.0 slice-done.3
  78.0 3.3 %fusion.10 = f32[256,2048]{1,0:T(8,128)S(1)} fusion(bf16[256,1792]{1,0:T(8,128)(2,1)} %get-tuple-element.5, bf16[2048,1792]{1,0:T(8,128)(2,1)S(1)} %bitcast.12), kind=kOutput, calls=%fused_computation.21 | convolution fusion | flops 1879048192 | bytes 10354688 | tf_op jit(solution)/shard_map/dot_general | solution.py:11
  81.3 3.5 %fusion = f32[256,2048]{1,0:T(8,128)} fusion(f32[256,2048]{1,0:T(8,128)S(1)} %fusion.10, bf16[256,1792]{1,0:T(8,128)(2,1)S(1)} %get-tuple-element.4, bf16[2048,1792]{1,0:T(8,128)(2,1)S(1)} %bitcast.14), kind=kOutput, calls=%fused_computation.7 | convolution fusion | flops 1880096768 | bytes 12451840 | tf_op jit(solution)/shard_map/dot_general | solution.py:11
  84.7 0.0 reduce-scatter.2.cloned.1.call-update
  84.8 0.0 copy-start.1
  84.8 5.2 %multiply_convert_fusion.1 = bf16[2048,1792]{1,0:T(8,128)(2,1)} fusion(bf16[256,1792]{1,0:T(8,128)(2,1)S(1)} %get-tuple-element.4, bf16[256,4096]{1,0:T(8,128)(2,1)S(1)} %copy-done), kind=kOutput, calls=%fused_computation.1 | convolution fusion | flops 1886388224 | bytes 9306112 | tf_op jit(solution)/shard_map/dot_general | solution.py:17
  90.0 0.0 copy-done.1
  90.0 5.4 %multiply_convert_fusion.2 = bf16[2048,1792]{1,0:T(8,128)(2,1)} fusion(bf16[256,1792]{1,0:T(8,128)(2,1)S(1)} %copy-done.1, bf16[256,4096]{1,0:T(8,128)(2,1)S(1)} %copy-done), kind=kOutput, calls=%fused_computation.2 | convolution fusion | flops 1886388224 | bytes 9306112 | tf_op jit(solution)/shard_map/dot_general | solution.py:17
  95.4 0.0 copy-done.3
  95.4 5.3 %multiply_convert_fusion = bf16[1792,2048]{1,0:T(8,128)(2,1)} fusion(bf16[256,4096]{1,0:T(8,128)(2,1)S(1)} %copy-done, f32[256,1792]{1,0:T(8,128)S(1)} %copy-done.3, f32[256,1792]{1,0:T(8,128)S(1)} %copy-done.2), kind=kOutput, calls=%fused_computation | convolution fusion | flops 1889140736 | bytes 12058624 | tf_op jit(solution)/shard_map/dot_general | solution.py:17
  100.7 26.8 %reduce-scatter.2.cloned.1.call-done = f32[64,2048]{1,0:T(8,128)} async-done(((f32[256,2048]{1,0:T(8,128)}), f32[64,2048]{1,0:T(8,128)}) %reduce-scatter.2.cloned.1.call-update) | async-done | bytes 524304 | tf_op jit(solution)/shard_map/reduce_scatter | solution.py:42
  127.5 1.8 %convert_element_type.23 = bf16[64,2048]{1,0:T(8,128)(2,1)} convert(f32[64,2048]{1,0:T(8,128)} %reduce-scatter.2.cloned.1.call-done) | non-fusion elementwise | flops 131072 | bytes 786432 | tf_op jit(solution)/shard_map/convert_element_type | solution.py:49
  (15 shorter events, 0.0 us)
Async XLA Ops:
  7.2 51.6 %all-gather.2.cloned.1.call-start = ((), (), s32[]{:S(2)}) async-start(), calls=%async_computation.1 | async-start | bytes 2621440 | tf_op jit(solution)/shard_map/all_gather | solution.py:24
  9.1 118.4 %reduce-scatter.2.cloned.1.call-start = ((), (), s32[]{:S(2)}) async-start(), calls=%async_computation.2 | async-start | bytes 2621440 | tf_op jit(solution)/shard_map/reduce_scatter | solution.py:42
  58.8 6.8 %copy-start = (bf16[256,4096]{1,0:T(8,128)(2,1)S(1)}, bf16[256,4096]{1,0:T(8,128)(2,1)}, u32[]{:S(2)}) copy-start(bf16[256,4096]{1,0:T(8,128)(2,1)} %all-gather.2.cloned.1.call-done) | copy-start | bytes 6291460
  58.8 13.4 %slice-start = ((s8[7340032]{0:T(1024)(128)(4,1)}), s8[4194304]{0:T(1024)(128)(4,1)S(1)}, s32[]{:S(2)}) async-start(s8[7340032]{0:T(1024)(128)(4,1)} %bitcast.9), calls=%async_computation.3 | async-start | bytes 8388608
  65.7 6.5 %slice-start.1 = ((s8[7340032]{0:T(1024)(128)(4,1)}), s8[3145728]{0:T(1024)(128)(4,1)S(1)}, s32[]{:S(2)}) async-start(s8[7340032]{0:T(1024)(128)(4,1)} %bitcast.9), calls=%async_computation.4 | async-start | bytes 6291456
  65.7 12.3 %slice-start.2 = ((s8[7340032]{0:T(1024)(128)(4,1)}), s8[4194304]{0:T(1024)(128)(4,1)S(1)}, s32[]{:S(2)}) async-start(s8[7340032]{0:T(1024)(128)(4,1)} %bitcast.11), calls=%async_computation.5 | async-start | bytes 8388608
  65.7 15.6 %slice-start.4 = ((s8[7340032]{0:T(1024)(128)(4,1)}), s8[4194304]{0:T(1024)(128)(4,1)S(1)}, s32[]{:S(2)}) async-start(s8[7340032]{0:T(1024)(128)(4,1)} %bitcast.13), calls=%async_computation.7 | async-start | bytes 8388608
  72.2 5.8 %slice-start.3 = ((s8[7340032]{0:T(1024)(128)(4,1)}), s8[3145728]{0:T(1024)(128)(4,1)S(1)}, s32[]{:S(2)}) async-start(s8[7340032]{0:T(1024)(128)(4,1)} %bitcast.11), calls=%async_computation.6 | async-start | bytes 6291456
  72.2 9.1 %slice-start.5 = ((s8[7340032]{0:T(1024)(128)(4,1)}), s8[3145728]{0:T(1024)(128)(4,1)S(1)}, s32[]{:S(2)}) async-start(s8[7340032]{0:T(1024)(128)(4,1)} %bitcast.13), calls=%async_computation.8 | async-start | bytes 6291456
  84.8 5.2 %copy-start.1 = (bf16[256,1792]{1,0:T(8,128)(2,1)S(1)}, bf16[256,1792]{1,0:T(8,128)(2,1)}, u32[]{:S(2)}) copy-start(bf16[256,1792]{1,0:T(8,128)(2,1)} %get-tuple-element.5) | copy-start | bytes 2752516
  90.0 5.4 %copy-start.2 = (f32[256,1792]{1,0:T(8,128)S(1)}, f32[256,1792]{1,0:T(8,128)}, u32[]{:S(2)}) copy-start(f32[256,1792]{1,0:T(8,128)} %convolution_multiply_fusion) | copy-start | bytes 5505028
  90.0 5.4 %copy-start.3 = (f32[256,1792]{1,0:T(8,128)S(1)}, f32[256,1792]{1,0:T(8,128)}, u32[]{:S(2)}) copy-start(f32[256,1792]{1,0:T(8,128)} %convolution_multiply_fusion.1) | copy-start | bytes 5505028
Sparse Core Ops, SparseCore 0:
  10.1 48.6 all-gather.1
  84.9 42.5 reduce-scatter.1
